TPU v7x, 32 devices: a whole 2x2x4 slice. The times are simulated.
32 devices in a mesh: row: 8 (over y, x, core), col: 4 (over z).
Axes of the slice: x: 2, y: 2, z: 4, core: 2. Of those that a mesh axis runs over, the one named last changes fastest.
Arguments:
- legendre: bfloat16 [4, 128, 89, 8, 128], P(None, 'col', None, 'row'), may hold values from -6 to 6
- longitude: float32 [512], replicated, may hold values from -3.140625 to 3.140625
- obs_weight: float32 [512], replicated, may hold values from 0.1 to 1.9
- span_weight: float32 [8], replicated, may hold values from 0.3 to 3
- span_of: int32 [512], replicated, may hold values from 0 to 7
- tile_order: int32 [712], replicated, may hold values from 0 to 711, each once
- slab_start: int32 [1], replicated, may hold values from 0 to 704
- resident: float32 [89, 8, 4, 128, 128], P(None, 'row', 'col'), may hold values from -6 to 6
Outputs:
- updated: float32 [89, 8, 4, 128, 128], P(None, 'row', 'col')
Inputs may be any that keep to these rules, and one draw needn't show every extreme that they name: tile_order is a permutation of the slot positions.
All inputs are finite; a program needn't handle non-finite values.
Results may differ from a plain program's by a relative error of at most 0.00074.
Values may be sent and summed in bfloat16 or wider, within the bound.
No kernel may reach another device: no remote copies, remote signals or barrier semaphores. Data moves between devices by JAX's collectives and lax.ppermute only.
A program may use at most 64 MiB of HBM per device.

v0:
```python
import math
import jax
import jax.numpy as jnp
from jax import lax
from jax.sharding import PartitionSpec as P

DEGREE = 300
UNK = 90600


def lookup_weights(obs_weight, span_weight, span_of):
    group_count = span_weight.shape[0]
    matches = span_of[:, None] == jnp.arange(group_count, dtype=jnp.int32)[None, :]
    factor = jnp.sum(jnp.where(matches, span_weight[None, :], 0.0), axis=1)
    return obs_weight * factor * (0.25 / math.sqrt(obs_weight.shape[0]))


def locate(tile_order, targets):
    places = jnp.arange(tile_order.shape[0], dtype=jnp.int32)
    return jnp.sum(jnp.where(tile_order[None, :] == targets[:, None], places[None, :], 0), axis=1)


def contract_rows(left_side, right_side):
    return lax.dot_general(
        left_side, right_side, (((0,), (0,)), ((), ())), preferred_element_type=jnp.float32
    )


def per_device(
    legendre, longitude, obs_weight, span_weight, span_of, tile_order, slab_start, resident
):
    block_count, shard_rows, slot_count, _, tile_size = legendre.shape
    row_count = lax.axis_size("row")
    col_count = lax.axis_size("col")
    row_index = lax.axis_index("row")
    col_index = lax.axis_index("col")
    block_rows = shard_rows * col_count
    order_map = tile_order.reshape(slot_count, row_count)
    own_tiles = lax.dynamic_slice_in_dim(order_map, row_index, 1, 1)[:, 0]
    unknown = own_tiles[:, None] * tile_size + jnp.arange(tile_size, dtype=jnp.int32)[None, :]
    orders = (unknown % (DEGREE + 1)).astype(jnp.float32).reshape(1, slot_count * tile_size)
    is_valid = (unknown < UNK).reshape(1, slot_count * tile_size)
    targets = slab_start[0] + jnp.arange(col_count, dtype=jnp.int32)
    positions = locate(tile_order, targets)
    target = targets[col_index]
    root_row = positions[col_index] % row_count
    root_slots = positions // row_count
    root_slot = root_slots[col_index]
    is_root = row_index == root_row
    weights = lookup_weights(obs_weight, span_weight, span_of).reshape(block_count, block_rows)
    angles = longitude.reshape(block_count, block_rows)
    in_lower = own_tiles >= target
    zero_piece = jnp.zeros((), jnp.bfloat16)
    all_values = legendre.reshape(block_count * shard_rows, slot_count * tile_size)
    own_angles = lax.dynamic_slice_in_dim(angles, col_index * shard_rows, shard_rows, 1)
    own_angles = own_angles.reshape(block_count * shard_rows)
    design_all = jnp.where(
        is_valid, all_values.astype(jnp.float32) * jnp.cos(own_angles[:, None] * orders), 0.0
    ).astype(jnp.bfloat16)
    design_all = design_all.reshape(block_count, shard_rows, slot_count * tile_size)
    gathered = lax.all_gather(design_all, "col", axis=1, tiled=True)
    gathered = gathered.reshape(block_count * block_rows, slot_count * tile_size)
    candidate = lax.dynamic_slice_in_dim(gathered, root_slot * tile_size, tile_size, 1)
    column = lax.psum(jnp.where(is_root, candidate, zero_piece), "row").astype(jnp.float32)
    weighted = (weights.reshape(block_count * block_rows)[:, None] * column).astype(jnp.bfloat16)
    running = contract_rows(gathered, weighted)
    update = jnp.where(
        in_lower[:, None, None], running.reshape(slot_count, tile_size, tile_size), 0.0
    )
    return resident + update.reshape(resident.shape)


def solution(mesh):
    placed = (
        P(None, "col", None, "row", None),
        P(),
        P(),
        P(),
        P(),
        P(),
        P(),
        P(None, "row", "col", None, None),
    )
    return jax.shard_map(
        per_device,
        mesh=mesh,
        in_specs=placed,
        out_specs=P(None, "row", "col", None, None),
        check_vma=False,
    )
```

profile of v0, /device:TPU:0, one launch (start us, length us, event | category | flops | bytes accessed | tf_op | source)
XLA Modules:
  0.0 322.1 jit_solution(3542823524447298766)
XLA Ops:
  6.5 0.0 copy-start
  6.5 0.0 all-gather.2.cloned.1.call-start
  6.5 0.8 reshape.90
  7.3 0.2 multiply_reduce_fusion
  7.5 0.1 fusion.4
  7.6 0.1 fusion.8
  7.7 5.5 %copy.20 = f32[4,32,89,1,128]{4,2,1,0,3:T(8,128)} copy(bf16[4,32,89,1,128]{4,1,3,2,0:T(8,128)(2,1)} %param.8) | data formatting | bytes 8749056 | tf_op jit(solution)/shard_map/convert_element_type | solution.py:58
  13.2 7.2 %reshape.94 = f32[4,32,11392]{2,1,0:T(8,128)} reshape(f32[4,32,89,1,128]{4,2,1,0,3:T(8,128)} %copy.20) | data formatting | bytes 11665408 | tf_op jit(solution)/shard_map/convert_element_type | solution.py:58
  20.4 0.0 copy-done
  20.4 0.1 constant_dynamic-slice_fusion
  20.5 0.0 copy-start.1
  20.5 0.0 copy-start.3
  20.5 0.0 copy-start.4
  20.5 0.0 copy-start.2
  20.5 22.0 %select_convert_fusion = bf16[4,32,11392]{2,1,0:T(8,128)(2,1)} fusion(f32[4,32,11392]{2,1,0:T(8,128)} %reshape.94, f32[11392]{0:T(1024)S(1)} %fusion.4, f32[4,32]{1,0:T(4,128)S(1)} %constant_dynamic-slice_fusion, pred[11392]{0:T(1024)(128)(4,1)S(1)} %fusion.8), kind=kLoop, calls=%fused_computation.2 | loop fusion | flops 5832704 | bytes 8806528 | tf_op jit(solution)/shard_map/convert_element_type | solution.py:59
  42.6 0.0 all-gather.2.cloned.1.call-update
  42.6 0.0 all-reduce.2.cloned.1.call-start
  43.3 0.0 copy-done.1
  43.3 0.2 select_reduce_fusion.1
  43.5 0.6 dynamic_slice.21
  46.0 0.6 dynamic_slice.22
  47.3 0.0 copy-done.3
  47.3 0.0 copy-done.4
  47.3 0.1 select_reduce_fusion
  47.4 201.2 %all-gather.2.cloned.1.call-done = bf16[4,128,11392]{2,1,0:T(8,128)(2,1)} async-done(((bf16[4,32,11392]{2,1,0:T(8,128)(2,1)}), bf16[4,128,11392]{2,1,0:T(8,128)(2,1)}) %all-gather.2.cloned.1.call-update) | async-done | bytes 11665424 | tf_op jit(solution)/shard_map/all_gather | solution.py:61
  248.6 1.6 dynamic-slice_select_fusion
  250.2 0.0 all-reduce.2.cloned.1.call-update
  250.3 0.0 copy-done.2
  250.3 0.6 dynamic_slice.19
  250.9 0.8 compare_reduce_fusion
  251.7 16.2 %copy.21 = bf16[11392,512]{1,0:T(8,128)(2,1)} copy(bf16[11392,512]{0,1:T(8,128)(2,1)} %bitcast.39) | data formatting | bytes 23330816 | tf_op jit(solution)/shard_map/dot_general | solution.py:24
  267.9 35.4 %all-reduce.2.cloned.1.call-done = bf16[512,128]{1,0:T(8,128)(2,1)} async-done(((bf16[512,128]{1,0:T(8,128)(2,1)}), bf16[512,128]{1,0:T(8,128)(2,1)}) %all-reduce.2.cloned.1.call-update) | async-done | bytes 131088 | tf_op jit(solution)/shard_map/psum | solution.py:64
  303.3 11.9 %fusion = f32[89,1,1,128,128]{4,3,2,1,0:T(8,128)} fusion(f32[89,1,1,128,128]{4,3,2,1,0:T(8,128)} %param.15, pred[89]{0:T(512)(128)(4,1)S(1)} %compare_reduce_fusion, bf16[89,128,512]{2,1,0:T(8,128)(2,1)} %bitcast.37, bf16[512,128]{1,0:T(8,128)(2,1)} %all-reduce.2.cloned.1.call-done, f32[512]{0:T(512)S(1)} %multiply_multiply_fusion), kind=kOutput, calls=%fused_computation.1 | convolution fusion | flops 1496285184 | bytes 23464024 | tf_op jit(solution)/shard_map/dot_general | solution.py:24
  (3 shorter events, 0.0 us)
Async XLA Ops:
  6.5 13.9 %copy-start = (f32[512]{0:T(512)S(1)}, f32[512]{0:T(512)}, u32[]{:S(2)}) copy-start(f32[512]{0:T(512)} %param.9) | copy-start | bytes 6148
  6.5 242.1 %all-gather.2.cloned.1.call-start = ((), (), s32[]{:S(2)}) async-start(), calls=%async_computation | async-start | bytes 14581760 | tf_op jit(solution)/shard_map/all_gather | solution.py:61
  20.5 22.8 %copy-start.1 = (s32[712]{0:T(1024)S(1)}, s32[712]{0:T(1024)}, u32[]{:S(2)}) copy-start(s32[712]{0:T(1024)} %param.13) | copy-start | bytes 8548
  20.5 26.8 %copy-start.3 = (s32[512]{0:T(512)S(1)}, s32[512]{0:T(512)}, u32[]{:S(2)}) copy-start(s32[512]{0:T(512)} %param.12) | copy-start | bytes 6148
  20.5 26.8 %copy-start.4 = (f32[8]{0:T(128)S(1)}, f32[8]{0:T(128)}, u32[]{:S(2)}) copy-start(f32[8]{0:T(128)} %param.11) | copy-start | bytes 100
  20.5 229.8 %copy-start.2 = (f32[512]{0:T(512)S(1)}, f32[512]{0:T(512)}, u32[]{:S(2)}) copy-start(f32[512]{0:T(512)} %param.10) | copy-start | bytes 6148
  42.6 260.7 %all-reduce.2.cloned.1.call-start = ((), (), s32[]{:S(2)}) async-start(), calls=%async_computation.1 | async-start | bytes 262144 | tf_op jit(solution)/shard_map/psum | solution.py:64
Sparse Core Ops, SparseCore 0:
  42.7 205.8 all-gather.1
  251.7 51.6 all-reduce.1
where the time goes:
time: 323 us; the launch traced here: 322 us
  waiting for transfers between devices  237 us (73%)
  local copies, waits for them, and re-layouts  31.5 us (10%)
  other arithmetic  25.1 us (8%)
  between operations  16.8 us (5%)
  matrix products  11.9 us (4%)
    all_gather x1, waiting for transfers between devices, per_device(): gathered = lax.all_gather(design_all, 'col', axis=1, tiled=True)  201 us
    psum x1, waiting for transfers between devices, per_device(): lax.psum(jnp.where(is_root, candidate, zero_piece), 'row')  35.4 us
    convert_element_type x1, other arithmetic, per_device(): design_all = jnp.where(is_valid, all_values.astype(jnp.float32) * jnp.cos...  22 us
    dot_general x1, local copies, waits for them, and re-layouts, contract_rows(): lax.dot_general(left_side, right_side, (((0,), (0,)), ((), ())), preferre...  16.2 us
    convert_element_type x2, local copies, waits for them, and re-layouts, per_device(): all_values.astype(jnp.float32) * jnp.cos(own_angles[:, None] * orders)  12.7 us
    dot_general x1, matrix products, contract_rows(): lax.dot_general(left_side, right_side, (((0,), (0,)), ((), ())), preferre...  11.9 us
  transfers between devices with their start and end apart: 2, of which 2 were waited for; matrix products, arithmetic and copies ran while one was open for 6% of the time, Pallas kernels for 0%

commit v1 on v0

--- a/solution.py
+++ b/solution.py
@@ -6,6 +6,12 @@
 
 DEGREE = 300
 UNK = 90600
+
+
+def add_all(shard, name):
+    parts = lax.all_gather(shard, name, axis=0, tiled=False)
+    total = parts.sum(axis=0)
+    return total
 
 
 def lookup_weights(obs_weight, span_weight, span_of):
@@ -61,7 +67,7 @@
     gathered = lax.all_gather(design_all, "col", axis=1, tiled=True)
     gathered = gathered.reshape(block_count * block_rows, slot_count * tile_size)
     candidate = lax.dynamic_slice_in_dim(gathered, root_slot * tile_size, tile_size, 1)
-    column = lax.psum(jnp.where(is_root, candidate, zero_piece), "row").astype(jnp.float32)
+    column = add_all(jnp.where(is_root, candidate, zero_piece), "row").astype(jnp.float32)
     weighted = (weights.reshape(block_count * block_rows)[:, None] * column).astype(jnp.bfloat16)
     running = contract_rows(gathered, weighted)
     update = jnp.where(

time: 323 us -> 293 us (0.907)
  waiting for transfers between devices: 237 us -> 206 us
    psum x1 -> x0, waiting for transfers between devices: 35.4 us -> none  [per_device(): lax.psum(jnp.where(is_root, candidate, zero_piece), 'row')]
    dot_general x1 -> x0, local copies, waits for them, and re-layouts: 16.2 us -> none  [contract_rows(): lax.dot_general(left_side, right_side, (((0,), (0,)), ((), ())), preferre...]
    reshape x0 -> x1, local copies, waits for them, and re-layouts: none -> 16.2 us  [per_device(): gathered.reshape(block_count * block_rows, slot_count * tile_size)]
    all_gather x0 -> x1, waiting for transfers between devices: none -> 4.16 us  [add_all(): parts = lax.all_gather(shard, name, axis=0, tiled=False)]
  transfers between devices with their start and end apart: 2 -> 2, of which waited for: 2 -> 2; matrix products, arithmetic and copies ran while one was open for 6% -> 7% of each run, Pallas kernels for 0% -> 0%
where the time goes in v1:
time: 293 us; the launch traced here: 292 us
  waiting for transfers between devices  206 us (70%)
  local copies, waits for them, and re-layouts  31.5 us (11%)
  other arithmetic  26.5 us (9%)
  between operations  16.8 us (6%)
  matrix products  11.8 us (4%)
    all_gather x1, waiting for transfers between devices, per_device(): gathered = lax.all_gather(design_all, 'col', axis=1, tiled=True)  201 us
    convert_element_type x1, other arithmetic, per_device(): design_all = jnp.where(is_valid, all_values.astype(jnp.float32) * jnp.cos...  22 us
    reshape x1, local copies, waits for them, and re-layouts, per_device(): gathered.reshape(block_count * block_rows, slot_count * tile_size)  16.2 us
    convert_element_type x2, local copies, waits for them, and re-layouts, per_device(): all_values.astype(jnp.float32) * jnp.cos(own_angles[:, None] * orders)  12.7 us
    dot_general x1, matrix products, contract_rows(): lax.dot_general(left_side, right_side, (((0,), (0,)), ((), ())), preferre...  11.8 us
  transfers between devices with their start and end apart: 2, of which 2 were waited for; matrix products, arithmetic and copies ran while one was open for 7% of the time, Pallas kernels for 0%

profile of v1, /device:TPU:0, one launch (start us, length us, event | category | flops | bytes accessed | tf_op | source)
XLA Modules:
  0.0 292.2 jit_solution(13314810340058614182)
XLA Ops:
  6.5 0.0 copy-start
  6.5 0.0 all-gather.4.cloned.1.call-start
  6.5 0.8 reshape.90
  7.3 0.2 multiply_reduce_fusion
  7.5 0.1 fusion.4
  7.6 0.1 fusion.8
  7.7 5.5 %copy.19 = f32[4,32,89,1,128]{4,2,1,0,3:T(8,128)} copy(bf16[4,32,89,1,128]{4,1,3,2,0:T(8,128)(2,1)} %param.8) | data formatting | bytes 8749056 | tf_op jit(solution)/shard_map/convert_element_type | solution.py:64
  13.2 7.2 %reshape.94 = f32[4,32,11392]{2,1,0:T(8,128)} reshape(f32[4,32,89,1,128]{4,2,1,0,3:T(8,128)} %copy.19) | data formatting | bytes 11665408 | tf_op jit(solution)/shard_map/convert_element_type | solution.py:64
  20.4 0.0 copy-done
  20.4 0.1 constant_dynamic-slice_fusion
  20.5 0.0 copy-start.1
  20.5 0.0 copy-start.3
  20.5 0.0 copy-start.4
  20.5 0.0 copy-start.2
  20.5 22.0 %select_convert_fusion = bf16[4,32,11392]{2,1,0:T(8,128)(2,1)} fusion(f32[4,32,11392]{2,1,0:T(8,128)} %reshape.94, f32[11392]{0:T(1024)S(1)} %fusion.4, f32[4,32]{1,0:T(4,128)S(1)} %constant_dynamic-slice_fusion, pred[11392]{0:T(1024)(128)(4,1)S(1)} %fusion.8), kind=kLoop, calls=%fused_computation.2 | loop fusion | flops 5832704 | bytes 8806528 | tf_op jit(solution)/shard_map/convert_element_type | solution.py:65
  42.6 0.0 all-gather.4.cloned.1.call-update
  42.6 0.0 all-gather.6.cloned.1.call-start
  43.3 0.0 copy-done.1
  43.3 0.2 select_reduce_fusion.1
  43.5 0.6 dynamic_slice.21
  46.0 0.6 dynamic_slice.22
  47.3 201.3 %all-gather.4.cloned.1.call-done = bf16[4,128,11392]{2,1,0:T(8,128)(2,1)} async-done(((bf16[4,32,11392]{2,1,0:T(8,128)(2,1)}), bf16[4,128,11392]{2,1,0:T(8,128)(2,1)}) %all-gather.4.cloned.1.call-update) | async-done | bytes 11665424 | tf_op jit(solution)/shard_map/all_gather | solution.py:67
  248.6 1.6 dynamic-slice_select_fusion
  250.2 0.0 all-gather.6.cloned.1.call-update
  250.3 0.6 dynamic_slice.19
  250.9 0.8 compare_reduce_fusion
  251.7 0.0 copy-done.3
  251.7 0.0 copy-done.4
  251.7 0.1 select_reduce_fusion
  251.8 0.0 copy-done.2
  251.8 16.2 %copy.20 = bf16[512,11392]{0,1:T(8,128)(2,1)} copy(bf16[512,11392]{1,0:T(8,128)(2,1)} %bitcast.40) | data formatting | bytes 23330816 | tf_op jit(solution)/shard_map/reshape | solution.py:68
  268.0 4.2 %all-gather.6.cloned.1.call-done = bf16[4096,128]{1,0:T(8,128)(2,1)} async-done(((bf16[512,128]{1,0:T(8,128)(2,1)}), bf16[4096,128]{1,0:T(8,128)(2,1)}) %all-gather.6.cloned.1.call-update) | async-done | bytes 1048592 | tf_op jit(solution)/shard_map/all_gather | solution.py:12
  272.1 1.4 reduce_sum.32
  273.5 11.8 %fusion = f32[89,1,1,128,128]{4,3,2,1,0:T(8,128)} fusion(f32[89,1,1,128,128]{4,3,2,1,0:T(8,128)} %param.15, pred[89]{0:T(512)(128)(4,1)S(1)} %compare_reduce_fusion, bf16[89,128,512]{2,1,0:T(8,128)(2,1)} %bitcast.38, bf16[512,128]{1,0:T(8,128)(2,1)S(1)} %reduce_sum.32, f32[512]{0:T(512)S(1)} %multiply_multiply_fusion), kind=kOutput, calls=%fused_computation.1 | convolution fusion | flops 1496285184 | bytes 23464024 | tf_op jit(solution)/shard_map/dot_general | solution.py:30
  (3 shorter events, 0.0 us)
Async XLA Ops:
  6.5 13.9 %copy-start = (f32[512]{0:T(512)S(1)}, f32[512]{0:T(512)}, u32[]{:S(2)}) copy-start(f32[512]{0:T(512)} %param.9) | copy-start | bytes 6148
  6.5 242.1 %all-gather.4.cloned.1.call-start = ((), (), s32[]{:S(2)}) async-start(), calls=%async_computation | async-start | bytes 14581760 | tf_op jit(solution)/shard_map/all_gather | solution.py:67
  20.5 22.8 %copy-start.1 = (s32[712]{0:T(1024)S(1)}, s32[712]{0:T(1024)}, u32[]{:S(2)}) copy-start(s32[712]{0:T(1024)} %param.13) | copy-start | bytes 8548
  20.5 231.2 %copy-start.3 = (s32[512]{0:T(512)S(1)}, s32[512]{0:T(512)}, u32[]{:S(2)}) copy-start(s32[512]{0:T(512)} %param.12) | copy-start | bytes 6148
  20.5 231.2 %copy-start.4 = (f32[8]{0:T(128)S(1)}, f32[8]{0:T(128)}, u32[]{:S(2)}) copy-start(f32[8]{0:T(128)} %param.11) | copy-start | bytes 100
  20.5 231.3 %copy-start.2 = (f32[512]{0:T(512)S(1)}, f32[512]{0:T(512)}, u32[]{:S(2)}) copy-start(f32[512]{0:T(512)} %param.10) | copy-start | bytes 6148
  42.6 229.5 %all-gather.6.cloned.1.call-start = ((), (), s32[]{:S(2)}) async-start(), calls=%async_computation.1 | async-start | bytes 1179648 | tf_op jit(solution)/shard_map/all_gather | solution.py:12
Sparse Core Ops, SparseCore 0:
  42.7 205.8 all-gather.3
  250.5 21.5 all-gather.5
